TPU v7x, 32 devices: a whole 2x2x4 slice. The times are simulated.
32 devices in a mesh: past: 4 (over y, x), second: 8 (over z, core).
Axes of the slice: x: 2, y: 2, z: 4, core: 2. Of those that a mesh axis runs over, the one named last changes fastest.
Arguments:
- resident: bfloat16 [12288, 12288], P('past', 'second'), may hold values from -6 to 6
- memory: bfloat16 [2, 384, 12288], P(None, None, 'past'), may hold values from -0.0546875 to 0.0546875
- previous: bfloat16 [2, 384, 12288], P(None, None, 'second'), may hold values from -6 to 6
- inverse_part: float32 [2, 384, 384], replicated, may hold values from -0.3125 to 0.3125
- pair_coupling: float32 [32, 32], replicated, may hold values from 0.0004510549 to 0.004510549
Outputs:
- fronts: bfloat16 [2, 384, 12288], P(None, None, 'second')
All inputs are finite; a program needn't handle non-finite values.
Results may differ from a plain program's by a relative error of at most 0.017.
Values may be sent and summed in bfloat16 or wider, within the bound.
A program may use at most 128 MiB of HBM per device.

v0:
```python
import jax
import jax.numpy as jnp
from jax import lax
from jax.sharding import PartitionSpec as P

step_size = 0.5


def orbital_flip(block, orbitals):
    row_count, col_count = block.shape
    blocks = block.reshape(row_count // orbitals, orbitals, col_count // orbitals, orbitals)
    return blocks.transpose(0, 3, 2, 1).reshape(row_count, col_count)


def solve_front(summed, prior, inverse_block):
    source = prior.astype(jnp.float32) - step_size * summed
    solved = source + jnp.dot(
        inverse_block, source, precision=lax.Precision.HIGHEST, preferred_element_type=jnp.float32
    )
    return solved.astype(jnp.bfloat16)


def self_energy(front, pair_coupling):
    orbitals = pair_coupling.shape[0]
    row_count, col_count = front.shape
    values = front.astype(jnp.float32)
    mirror = orbital_flip(values, orbitals)
    blocks = (values * values * mirror).reshape(
        row_count // orbitals, orbitals, col_count // orbitals, orbitals
    )
    return (
        (blocks * pair_coupling[None, :, None, :])
        .reshape(row_count, col_count)
        .astype(jnp.bfloat16)
    )


def per_device(resident, memory, previous, inverse_part, pair_coupling):
    past_count = lax.axis_size("past")

    def advance(memory_row, front_index):
        partial_value = jnp.dot(memory_row, resident, preferred_element_type=jnp.float32)
        summed = lax.psum(partial_value.astype(jnp.bfloat16), "past").astype(jnp.float32)
        prior_cols = previous[front_index]
        return solve_front(summed, prior_cols, inverse_part[front_index])

    front_one = advance(memory[0], 0)
    energy_one = self_energy(front_one, pair_coupling)
    band = energy_one.shape[0] // past_count
    own_rows = lax.dynamic_slice_in_dim(energy_one, lax.axis_index("past") * band, band, 0)
    wide_band = lax.all_gather(own_rows, "second", axis=1, tiled=True)
    gathered = lax.all_to_all(wide_band, "past", split_axis=1, concat_axis=0, tiled=True)
    orbitals = pair_coupling.shape[0]
    memory_next = (
        memory[1].astype(jnp.float32) + orbital_flip(gathered, orbitals).astype(jnp.float32)
    ).astype(jnp.bfloat16)
    front_two = advance(memory_next, 1)
    return jnp.stack([front_one, front_two])


def solution(mesh):
    in_specs = (P("past", "second"), P(None, None, "past"), P(None, None, "second"), P(), P())
    out_specs = P(None, None, "second")
    return jax.shard_map(
        per_device, mesh=mesh, in_specs=in_specs, out_specs=out_specs, check_vma=False
    )
```

profile of v0, /device:TPU:0, one launch (start us, length us, event | category | flops | bytes accessed | tf_op | source)
XLA Modules:
  0.0 301.7 jit_solution(1481439341360291000)
XLA Ops:
  6.5 0.0 copy-start
  6.5 0.0 all-reduce.3.cloned.1.call-start
  6.5 9.2 %convolution_convert_fusion.1 = bf16[384,1536]{1,0:T(8,128)(2,1)} fusion(bf16[3072,1536]{1,0:T(8,128)(2,1)} %param.5, bf16[2,384,3072]{2,1,0:T(8,128)(2,1)} %param.6), kind=kOutput, calls=%fused_computation.10 | convolution fusion | flops 3624468480 | bytes 12976128 | tf_op jit(solution)/shard_map/dot_general | solution.py:42
  15.8 0.0 all-reduce.3.cloned.1.call-update
  15.8 0.0 all-gather.2.cloned.1.call-start
  15.8 0.0 copy-done
  15.9 4.4 %mul.29 = f32[12,32,48,32]{3,2,1,0:T(8,128)} broadcast(f32[32,32]{1,0:T(8,128)S(1)} %copy-done), dimensions={1,3} | broadcast | bytes 2363392 | tf_op jit(solution)/shard_map/mul | solution.py:32
  20.3 6.9 %mul.30 = f32[384,1536]{1,0:T(8,128)S(1)} reshape(f32[12,32,48,32]{3,2,1,0:T(8,128)} %mul.29) | data formatting | bytes 4718592 | tf_op jit(solution)/shard_map/mul | solution.py:32
  27.2 45.8 %all-reduce.3.cloned.1.call-done = bf16[384,1536]{1,0:T(8,128)(2,1)} async-done(((bf16[384,1536]{1,0:T(8,128)(2,1)}), bf16[384,1536]{1,0:T(8,128)(2,1)}) %all-reduce.3.cloned.1.call-update) | async-done | bytes 1179664 | tf_op jit(solution)/shard_map/psum | solution.py:43
  73.0 8.3 %fusion.28 = (f32[384,1536]{1,0:T(8,128)}, bf16[384,1536]{1,0:T(8,128)(2,1)S(1)}) fusion(f32[2,384,384]{2,1,0:T(8,128)} %param.8, bf16[384,1536]{1,0:T(8,128)(2,1)} %all-reduce.3.cloned.1.call-done, bf16[2,384,1536]{2,1,0:T(8,128)(2,1)} %param.7), kind=kOutput, calls=%fused_computation.40 | convolution fusion | flops 2724397056 | bytes 8847360 | tf_op jit(solution)/shard_map/dot_general | solution.py:17
  81.3 5.0 %reshape.26 = f32[12,32,48,32]{3,2,1,0:T(8,128)} reshape(bf16[384,1536]{1,0:T(8,128)(2,1)S(1)} %get-tuple-element.6) | data formatting | bytes 3538944 | tf_op jit(solution)/shard_map/reshape | solution.py:11
  86.3 10.8 %copy.8 = f32[12,32,48,32]{3,2,1,0:T(8,128)} copy(f32[12,32,48,32]{1,2,3,0:T(8,128)} %bitcast.65) | data formatting | bytes 4718592 | tf_op jit(solution)/shard_map/transpose | solution.py:12
  97.1 7.7 %reshape.27 = f32[384,1536]{1,0:T(8,128)} reshape(f32[12,32,48,32]{3,2,1,0:T(8,128)} %copy.8) | data formatting | bytes 4718592 | tf_op jit(solution)/shard_map/reshape | solution.py:12
  104.8 2.0 fusion.21
  106.9 0.0 all-gather.2.cloned.1.call-update
  106.9 0.0 all-reduce.5.cloned.1.call-start
  106.9 31.5 %all-gather.2.cloned.1.call-done = bf16[96,12288]{1,0:T(8,128)(2,1)} async-done(((bf16[96,1536]{1,0:T(8,128)(2,1)}), bf16[96,12288]{1,0:T(8,128)(2,1)}) %all-gather.2.cloned.1.call-update) | async-done | bytes 2359312 | tf_op jit(solution)/shard_map/all_gather | solution.py:51
  138.5 1.8 copy.15
  140.3 32.0 %all_to_all.13 = bf16[96,4,3072]{2,0,1:T(8,128)(2,1)S(1)} all-to-all(bf16[96,4,3072]{2,0,1:T(8,128)(2,1)S(1)} %bitcast.66), channel_id=1, replica_groups=mesh['past'=4,'second'=8] {'past'}, dimensions={1} | all-to-all | bytes 4718592 | tf_op jit(solution)/shard_map/all_to_all | solution.py:52
  172.4 2.7 convert_bitcast_fusion
  175.1 12.3 %reshape.32 = f32[12,32,96,32]{3,2,1,0:T(8,128)} reshape(f32[4,96,3072]{2,1,0:T(8,128)} %convert_bitcast_fusion) | data formatting | bytes 9437184 | tf_op jit(solution)/shard_map/convert_element_type | solution.py:55
  187.4 22.5 %copy.10 = f32[12,32,96,32]{3,2,1,0:T(8,128)} copy(f32[12,32,96,32]{1,2,3,0:T(8,128)} %bitcast.64) | data formatting | bytes 9437184 | tf_op jit(solution)/shard_map/convert_element_type | solution.py:55
  209.9 14.6 %reshape.31 = f32[384,3072]{1,0:T(8,128)} reshape(f32[12,32,96,32]{3,2,1,0:T(8,128)} %copy.10) | data formatting | bytes 9437184 | tf_op jit(solution)/shard_map/convert_element_type | solution.py:55
  224.4 0.0 copy-start.1
  224.5 10.7 %convolution_convert_fusion = bf16[384,1536]{1,0:T(8,128)(2,1)} fusion(bf16[3072,1536]{1,0:T(8,128)(2,1)} %param.5, f32[384,3072]{1,0:T(8,128)} %reshape.31, bf16[2,384,3072]{2,1,0:T(8,128)(2,1)} %param.6), kind=kOutput, calls=%fused_computation.9 | convolution fusion | flops 3628007424 | bytes 17694720 | tf_op jit(solution)/shard_map/dot_general | solution.py:42
  235.2 0.0 all-reduce.5.cloned.1.call-update
  235.2 52.3 %all-reduce.5.cloned.1.call-done = bf16[384,1536]{1,0:T(8,128)(2,1)} async-done(((bf16[384,1536]{1,0:T(8,128)(2,1)}), bf16[384,1536]{1,0:T(8,128)(2,1)}) %all-reduce.5.cloned.1.call-update) | async-done | bytes 1179664 | tf_op jit(solution)/shard_map/psum | solution.py:43
  287.5 0.0 copy-done.1
  287.5 6.1 %fusion.5 = bf16[1,384,1536]{2,1,0:T(8,128)(2,1)S(1)} fusion(bf16[384,1536]{1,0:T(8,128)(2,1)} %all-reduce.5.cloned.1.call-done, bf16[2,384,1536]{2,1,0:T(8,128)(2,1)S(1)} %copy-done.1, f32[2,384,384]{2,1,0:T(8,128)} %param.8), kind=kOutput, calls=%fused_computation.11 | convolution fusion | flops 2723807232 | bytes 6488064 | tf_op jit(solution)/shard_map/dot_general | solution.py:17
  293.6 1.6 pad_maximum_fusion
Async XLA Ops:
  6.5 9.3 %copy-start = (f32[32,32]{1,0:T(8,128)S(1)}, f32[32,32]{1,0:T(8,128)}, u32[]{:S(2)}) copy-start(f32[32,32]{1,0:T(8,128)} %param.9) | copy-start | bytes 12292
  6.5 66.5 %all-reduce.3.cloned.1.call-start = ((), (), s32[]{:S(2)}) async-start(), calls=%async_computation.1 | async-start | bytes 2359296 | tf_op jit(solution)/shard_map/psum | solution.py:43
  15.8 122.7 %all-gather.2.cloned.1.call-start = ((), (), s32[]{:S(2)}) async-start(), calls=%async_computation.2 | async-start | bytes 2654208 | tf_op jit(solution)/shard_map/all_gather | solution.py:51
  106.9 180.6 %all-reduce.5.cloned.1.call-start = ((), (), s32[]{:S(2)}) async-start(), calls=%async_computation.3 | async-start | bytes 2359296 | tf_op jit(solution)/shard_map/psum | solution.py:43
  224.4 63.0 %copy-start.1 = (bf16[2,384,1536]{2,1,0:T(8,128)(2,1)S(1)}, bf16[2,384,1536]{2,1,0:T(8,128)(2,1)}, u32[]{:S(2)}) copy-start(bf16[2,384,1536]{2,1,0:T(8,128)(2,1)} %param.7) | copy-start | bytes 7077892
Sparse Core Ops, SparseCore 0:
  15.9 57.0 all-reduce.2
  107.0 31.4 all-gather.1
  235.3 52.1 all-reduce.4
where the time goes:
time: 303 us; the launch traced here: 302 us
  waiting for transfers between devices  130 us (43%)
  local copies, waits for them, and re-layouts  86.1 us (28%)
  matrix products  34.3 us (11%)
  blocking collectives  32 us (11%)
  between operations  13.2 us (4%)
  other arithmetic  6.39 us (2%)
    psum x2, waiting for transfers between devices, advance(): lax.psum(partial_value.astype(jnp.bfloat16), 'past').astype(jnp.float32)  98.1 us
    convert_element_type x3, local copies, waits for them, and re-layouts, per_device(): orbital_flip(gathered, orbitals).astype(jnp.float32)  49.4 us
    all_to_all x1, blocking collectives, per_device(): lax.all_to_all(wide_band, 'past', split_axis=1, concat_axis=0, tiled=True)  32 us
    all_gather x1, waiting for transfers between devices, per_device(): wide_band = lax.all_gather(own_rows, 'second', axis=1, tiled=True)  31.5 us
    dot_general x2, matrix products, advance(): jnp.dot(memory_row, resident, preferred_element_type=jnp.float32)  19.9 us
    dot_general x2, matrix products, solve_front(): jnp.dot(inverse_block, source, precision=lax.Precision.HIGHEST, preferred...  14.3 us
    mul x2, local copies, waits for them, and re-layouts, self_energy(): blocks * pair_coupling[None, :, None, :]  11.3 us
    transpose x1, local copies, waits for them, and re-layouts, orbital_flip(): return blocks.transpose(0, 3, 2, 1).reshape(row_count, col_count)  10.8 us
  transfers between devices with their start and end apart: 3, of which 3 were waited for; matrix products, arithmetic and copies ran while one was open for 4% of the time, Pallas kernels for 0%

commit v1 on v0

--- a/solution.py
+++ b/solution.py
@@ -4,6 +4,11 @@
 from jax.sharding import PartitionSpec as P
 
 step_size = 0.5
+
+
+def gather_and_add(value, name):
+    shards = lax.all_gather(value, name)
+    return jnp.sum(shards, axis=0)
 
 
 def orbital_flip(block, orbitals):
@@ -40,7 +45,7 @@
 
     def advance(memory_row, front_index):
         partial_value = jnp.dot(memory_row, resident, preferred_element_type=jnp.float32)
-        summed = lax.psum(partial_value.astype(jnp.bfloat16), "past").astype(jnp.float32)
+        summed = gather_and_add(partial_value.astype(jnp.bfloat16), "past").astype(jnp.float32)
         prior_cols = previous[front_index]
         return solve_front(summed, prior_cols, inverse_part[front_index])
 

time: 303 us -> 316 us (1.043)
  other arithmetic: 6.39 us -> 14.7 us
  waiting for transfers between devices: 130 us -> 135 us
    all_gather x0 -> x2, waiting for transfers between devices: none -> 103 us  [gather_and_add(): shards = lax.all_gather(value, name)]
    psum x2 -> x0, waiting for transfers between devices: 98.1 us -> none  [advance(): lax.psum(partial_value.astype(jnp.bfloat16), 'past').astype(jnp.float32)]
    reduce_sum x0 -> x2, other arithmetic: none -> 8.26 us  [gather_and_add(): return jnp.sum(shards, axis=0)]
where the time goes in v1:
time: 316 us; the launch traced here: 315 us
  waiting for transfers between devices  135 us (43%)
  local copies, waits for them, and re-layouts  86.1 us (27%)
  matrix products  34 us (11%)
  blocking collectives  32 us (10%)
  other arithmetic  14.7 us (5%)
  between operations  13.2 us (4%)
    all_gather x2, waiting for transfers between devices, gather_and_add(): shards = lax.all_gather(value, name)  103 us
    convert_element_type x3, local copies, waits for them, and re-layouts, per_device(): orbital_flip(gathered, orbitals).astype(jnp.float32)  49.4 us
    all_to_all x1, blocking collectives, per_device(): lax.all_to_all(wide_band, 'past', split_axis=1, concat_axis=0, tiled=True)  32 us
    all_gather x1, waiting for transfers between devices, per_device(): wide_band = lax.all_gather(own_rows, 'second', axis=1, tiled=True)  31.5 us
    dot_general x2, matrix products, advance(): jnp.dot(memory_row, resident, preferred_element_type=jnp.float32)  19.8 us
    dot_general x2, matrix products, solve_front(): jnp.dot(inverse_block, source, precision=lax.Precision.HIGHEST, preferred...  14.2 us
    mul x2, local copies, waits for them, and re-layouts, self_energy(): blocks * pair_coupling[None, :, None, :]  11.4 us
    transpose x1, local copies, waits for them, and re-layouts, orbital_flip(): return blocks.transpose(0, 3, 2, 1).reshape(row_count, col_count)  10.8 us
  transfers between devices with their start and end apart: 3, of which 3 were waited for; matrix products, arithmetic and copies ran while one was open for 4% of the time, Pallas kernels for 0%

profile of v1, /device:TPU:0, one launch (start us, length us, event | category | flops | bytes accessed | tf_op | source)
XLA Modules:
  0.0 314.9 jit_solution(1704897174596839564)
XLA Ops:
  6.5 0.0 copy-start
  6.5 0.0 all-gather.8.cloned.1.call-start
  6.5 9.2 %convolution_convert_fusion.1 = bf16[384,1536]{1,0:T(8,128)(2,1)} fusion(bf16[3072,1536]{1,0:T(8,128)(2,1)} %param.5, bf16[2,384,3072]{2,1,0:T(8,128)(2,1)} %param.6), kind=kOutput, calls=%fused_computation.14 | convolution fusion | flops 3624468480 | bytes 12976128 | tf_op jit(solution)/shard_map/dot_general | solution.py:47
  15.8 0.0 all-gather.8.cloned.1.call-update
  15.8 0.0 all-gather.6.cloned.1.call-start
  15.8 0.0 copy-done
  15.9 4.4 %mul.50 = f32[12,32,48,32]{3,2,1,0:T(8,128)} broadcast(f32[32,32]{1,0:T(8,128)S(1)} %copy-done), dimensions={1,3} | broadcast | bytes 2363392 | tf_op jit(solution)/shard_map/mul | solution.py:37
  20.3 6.9 %mul.51 = f32[384,1536]{1,0:T(8,128)S(1)} reshape(f32[12,32,48,32]{3,2,1,0:T(8,128)} %mul.50) | data formatting | bytes 4718592 | tf_op jit(solution)/shard_map/mul | solution.py:37
  27.2 48.4 %all-gather.8.cloned.1.call-done = bf16[1536,1536]{1,0:T(8,128)(2,1)} async-done(((bf16[384,1536]{1,0:T(8,128)(2,1)}), bf16[1536,1536]{1,0:T(8,128)(2,1)}) %all-gather.8.cloned.1.call-update) | async-done | bytes 4718608 | tf_op jit(solution)/shard_map/all_gather | solution.py:10
  75.6 4.4 %reduce_sum.24 = bf16[384,1536]{1,0:T(8,128)(2,1)} reduce(bf16[4,384,1536]{2,1,0:T(8,128)(2,1)} %bitcast.87, bf16[]{:T(256)} %constant.6.clone.1), dimensions={0}, to_apply=%region_0.0 | reduce | flops 1769472 | bytes 5898242 | tf_op jit(solution)/shard_map/reduce_sum | solution.py:11
  80.0 8.2 %fusion.34 = (f32[384,1536]{1,0:T(8,128)}, bf16[384,1536]{1,0:T(8,128)(2,1)S(1)}) fusion(f32[2,384,384]{2,1,0:T(8,128)} %param.8, bf16[384,1536]{1,0:T(8,128)(2,1)} %reduce_sum.24, bf16[2,384,1536]{2,1,0:T(8,128)(2,1)} %param.7), kind=kOutput, calls=%fused_computation.46 | convolution fusion | flops 2724397056 | bytes 8847360 | tf_op jit(solution)/shard_map/dot_general | solution.py:22
  88.3 5.0 %reshape.54 = f32[12,32,48,32]{3,2,1,0:T(8,128)} reshape(bf16[384,1536]{1,0:T(8,128)(2,1)S(1)} %get-tuple-element.6) | data formatting | bytes 3538944 | tf_op jit(solution)/shard_map/reshape | solution.py:16
  93.2 10.8 %copy.8 = f32[12,32,48,32]{3,2,1,0:T(8,128)} copy(f32[12,32,48,32]{1,2,3,0:T(8,128)} %bitcast.85) | data formatting | bytes 4718592 | tf_op jit(solution)/shard_map/transpose | solution.py:17
  104.1 7.7 %reshape.55 = f32[384,1536]{1,0:T(8,128)} reshape(f32[12,32,48,32]{3,2,1,0:T(8,128)} %copy.8) | data formatting | bytes 4718592 | tf_op jit(solution)/shard_map/reshape | solution.py:17
  111.8 2.0 fusion.27
  113.8 0.0 all-gather.6.cloned.1.call-update
  113.9 0.0 all-gather.10.cloned.1.call-start
  113.9 31.5 %all-gather.6.cloned.1.call-done = bf16[96,12288]{1,0:T(8,128)(2,1)} async-done(((bf16[96,1536]{1,0:T(8,128)(2,1)}), bf16[96,12288]{1,0:T(8,128)(2,1)}) %all-gather.6.cloned.1.call-update) | async-done | bytes 2359312 | tf_op jit(solution)/shard_map/all_gather | solution.py:56
  145.5 1.8 copy.15
  147.3 32.0 %all_to_all.13 = bf16[96,4,3072]{2,0,1:T(8,128)(2,1)S(1)} all-to-all(bf16[96,4,3072]{2,0,1:T(8,128)(2,1)S(1)} %bitcast.86), channel_id=1, replica_groups=mesh['past'=4,'second'=8] {'past'}, dimensions={1} | all-to-all | bytes 4718592 | tf_op jit(solution)/shard_map/all_to_all | solution.py:57
  179.3 2.7 convert_bitcast_fusion
  182.1 12.3 %reshape.60 = f32[12,32,96,32]{3,2,1,0:T(8,128)} reshape(f32[4,96,3072]{2,1,0:T(8,128)} %convert_bitcast_fusion) | data formatting | bytes 9437184 | tf_op jit(solution)/shard_map/convert_element_type | solution.py:60
  194.4 22.5 %copy.10 = f32[12,32,96,32]{3,2,1,0:T(8,128)} copy(f32[12,32,96,32]{1,2,3,0:T(8,128)} %bitcast.84) | data formatting | bytes 9437184 | tf_op jit(solution)/shard_map/convert_element_type | solution.py:60
  216.9 14.6 %reshape.59 = f32[384,3072]{1,0:T(8,128)} reshape(f32[12,32,96,32]{3,2,1,0:T(8,128)} %copy.10) | data formatting | bytes 9437184 | tf_op jit(solution)/shard_map/convert_element_type | solution.py:60
  231.4 10.6 %convolution_convert_fusion = bf16[384,1536]{1,0:T(8,128)(2,1)} fusion(bf16[3072,1536]{1,0:T(8,128)(2,1)} %param.5, f32[384,3072]{1,0:T(8,128)} %reshape.59, bf16[2,384,3072]{2,1,0:T(8,128)(2,1)} %param.6), kind=kOutput, calls=%fused_computation.13 | convolution fusion | flops 3628007424 | bytes 17694720 | tf_op jit(solution)/shard_map/dot_general | solution.py:47
  242.0 0.0 all-gather.10.cloned.1.call-update
  242.0 54.9 %all-gather.10.cloned.1.call-done = bf16[1536,1536]{1,0:T(8,128)(2,1)} async-done(((bf16[384,1536]{1,0:T(8,128)(2,1)}), bf16[1536,1536]{1,0:T(8,128)(2,1)}) %all-gather.10.cloned.1.call-update) | async-done | bytes 4718608 | tf_op jit(solution)/shard_map/all_gather | solution.py:10
  296.9 0.0 copy-start.1
  296.9 3.8 %reduce_sum.25 = bf16[384,1536]{1,0:T(8,128)(2,1)S(1)} reduce(bf16[4,384,1536]{2,1,0:T(8,128)(2,1)} %bitcast.88, bf16[]{:T(256)} %constant.6.clone.1), dimensions={0}, to_apply=%region_1.0 | reduce | flops 1769472 | bytes 5898242 | tf_op jit(solution)/shard_map/reduce_sum | solution.py:11
  300.7 0.0 copy-done.1
  300.8 6.0 %fusion.5 = bf16[1,384,1536]{2,1,0:T(8,128)(2,1)S(1)} fusion(bf16[384,1536]{1,0:T(8,128)(2,1)S(1)} %reduce_sum.25, bf16[2,384,1536]{2,1,0:T(8,128)(2,1)} %param.7, f32[2,384,384]{2,1,0:T(8,128)S(1)} %copy-done.1), kind=kOutput, calls=%fused_computation.15 | convolution fusion | flops 2723807232 | bytes 6488064 | tf_op jit(solution)/shard_map/dot_general | solution.py:22
  306.8 1.6 pad_maximum_fusion
Async XLA Ops:
  6.5 9.3 %copy-start = (f32[32,32]{1,0:T(8,128)S(1)}, f32[32,32]{1,0:T(8,128)}, u32[]{:S(2)}) copy-start(f32[32,32]{1,0:T(8,128)} %param.9) | copy-start | bytes 12292
  6.5 69.1 %all-gather.8.cloned.1.call-start = ((), (), s32[]{:S(2)}) async-start(), calls=%async_computation.2 | async-start | bytes 5898240 | tf_op jit(solution)/shard_map/all_gather | solution.py:10
  15.8 129.7 %all-gather.6.cloned.1.call-start = ((), (), s32[]{:S(2)}) async-start(), calls=%async_computation.1 | async-start | bytes 2654208 | tf_op jit(solution)/shard_map/all_gather | solution.py:56
  113.9 183.0 %all-gather.10.cloned.1.call-start = ((), (), s32[]{:S(2)}) async-start(), calls=%async_computation.3 | async-start | bytes 5898240 | tf_op jit(solution)/shard_map/all_gather | solution.py:10
  296.9 3.8 %copy-start.1 = (f32[2,384,384]{2,1,0:T(8,128)S(1)}, f32[2,384,384]{2,1,0:T(8,128)}, u32[]{:S(2)}) copy-start(f32[2,384,384]{2,1,0:T(8,128)} %param.8) | copy-start | bytes 3538948
Sparse Core Ops, SparseCore 0:
  15.9 59.6 all-gather.7
  114.0 31.4 all-gather.5
  242.1 54.7 all-gather.9
